TPU v7x, 32 devices: a whole 2x2x4 slice. The times are simulated.
32 devices in a mesh: groups: 2 (over x), mix: 16 (over z, y, core).
Axes of the slice: x: 2, y: 2, z: 4, core: 2. Of those that a mesh axis runs over, the one named last changes fastest.
Arguments:
- resid_in: bfloat16 [4096, 2048], P(('groups', 'mix')), parts along dimension 0, may hold values from -40 to 40
- head_in: bfloat16 [4096, 4096], P('groups', 'mix'), parts along dimension 0, may hold values from -6 to 6
- gate_in: bfloat16 [4096, 4096], P('groups', 'mix'), parts along dimension 0, may hold values from -64 to 64
- in_basis: bfloat16 [4096, 128], P('groups'), parts along dimension 0, may hold values from -6 to 6
- out_basis: bfloat16 [4096, 128], P('groups'), parts along dimension 0, may hold values from -6 to 6
- step_size: float32 [64, 4096], P('mix', 'groups'), parts along dimension 1, may hold values from 0 to 2
- decay_rate: float32 [64], P('mix'), may hold values from 0.5 to 2
- init_state: float32 [16, 64, 64, 128], P('groups', 'mix'), parts along dimension 0, may hold values from -0.6 to 0.6
- lengths: int32 [16], P('groups'), parts along dimension 0, may hold values from 1 to 512, 2048 in all
- norm_gain: float32 [4096], replicated, may hold values from 0.1 to 1.9
- out_proj: bfloat16 [4096, 2048], P('mix'), may hold values from -0.09375 to 0.09375
- moe_gain: float32 [2048], replicated, may hold values from 0.1 to 1.9
- expert_ids: int32 [4096, 8], P(('groups', 'mix')), parts along dimension 0, may hold values from 0 to 31, as said below
- route_weight: float32 [4096, 8], P(('groups', 'mix')), parts along dimension 0, may hold values from 0.1 to 0.4
- placement: int32 [32], replicated, may hold values from 0 to 31, each once
- w_gate: bfloat16 [32, 2048, 768], P('mix'), may hold values from -0.125 to 0.125
- w_up: bfloat16 [32, 2048, 768], P('mix'), may hold values from -0.125 to 0.125
- w_down: bfloat16 [32, 768, 2048], P('mix'), may hold values from -0.21875 to 0.21875
Outputs:
- layer_out: bfloat16 [4096, 2048], P(('groups', 'mix')), parts along dimension 0
There are 2 independent parts, one for each index of `groups`. A program takes and returns all parts, laid end to end along the dimension named above; an argument that names none is the same for every part. Nothing has to cross between parts.
Inputs may be any that keep to these rules, and one draw needn't show every extreme that they name: `expert_ids`: each row names 8 different experts. Within each aligned block of 128 rows (one device's rows), 8 experts appear exactly 64 times each, 8 others 64 / 2 times each and the rest 64 / 4 times each; each of the three sets is the same in every block. `placement`: each slot once. `lengths`: requests fill the 2048 positions in order.
All inputs are finite; a program needn't handle non-finite values.
Results may differ from a plain program's by a relative error of at most 0.013.
Values may be sent and summed in bfloat16 or wider, within the bound.
No kernel may reach another device: no remote copies, remote signals or barrier semaphores. Data moves between devices by JAX's collectives and lax.ppermute only.
A program may use at most 128 MiB of HBM per device.

v0:
```python
import jax
import jax.numpy as jnp
from jax import lax
from jax.sharding import PartitionSpec as P

HEADS = 64
HEAD_DIM = 64
SPAN = 256
epsilon = 1e-05


def request_layout(lengths, tokens_total):
    request_end = jnp.cumsum(lengths)
    request_first = request_end - lengths
    position = jnp.arange(tokens_total, dtype=jnp.int32)
    segment = jnp.sum((position[None, :] >= request_end[:, None]).astype(jnp.int32), axis=0)
    member = segment[None, :] == jnp.arange(lengths.shape[0], dtype=jnp.int32)[:, None]
    first_of = jnp.sum(jnp.where(member, request_first[:, None], 0), axis=0)
    return (segment, first_of, member)


def scan_heads(
    head_values,
    head_steps,
    head_rates,
    in_basis,
    out_basis,
    state_init,
    segment,
    first_of,
    member,
    block_len,
):
    tokens_total = head_values.shape[0]
    local_heads = head_steps.shape[0]
    head_width = head_values.shape[1] // local_heads
    blocks = tokens_total // block_len
    highest = lax.Precision.HIGHEST
    log_decay = -head_steps * head_rates[:, None]
    driven = (
        head_values.reshape(tokens_total, local_heads, head_width)
        .transpose(1, 0, 2)
        .astype(jnp.float32)
    )
    driven = driven * head_steps[:, :, None]
    drive_split = driven.reshape(local_heads, blocks, block_len, head_width).transpose(1, 0, 2, 3)
    decay_split = log_decay.reshape(local_heads, blocks, block_len).transpose(1, 0, 2)

    def split_rows(array):
        return array.reshape((blocks, block_len) + array.shape[1:])

    block_first = jnp.arange(blocks, dtype=jnp.int32) * block_len
    member_blocks = member.reshape(member.shape[0], blocks, block_len).transpose(1, 0, 2)
    init_heads = state_init.transpose(1, 0, 2, 3)
    inputs = (
        drive_split,
        decay_split,
        split_rows(in_basis),
        split_rows(out_basis),
        split_rows(segment),
        split_rows(first_of),
        member_blocks,
        block_first,
    )
    offsets = jnp.arange(block_len, dtype=jnp.int32)
    causal = offsets[None, :] <= offsets[:, None]

    def advance(states_in, block_in):
        (
            drive_heads,
            decay_heads,
            basis_block,
            readout_block,
            segment_block,
            first_block,
            member_block,
            first_pos,
        ) = block_in
        basis_wide = basis_block.astype(jnp.float32)
        readout_wide = readout_block.astype(jnp.float32)
        same_seq = (segment_block[:, None] == segment_block[None, :]) & causal
        scores = jnp.dot(readout_block, basis_block.T, preferred_element_type=jnp.float32)
        carried = first_block < first_pos
        member_wide = member_block.astype(jnp.float32)

        def one_head(state_in, drive_block, decay_block, head_init):
            running = jnp.cumsum(decay_block)
            earlier = running - decay_block
            gap_values = jnp.minimum(running[:, None] - running[None, :], 0.0)
            kernel = jnp.where(same_seq, jnp.exp(gap_values), 0.0)
            output = jnp.dot(kernel * scores, drive_block, precision=highest)
            before = jnp.max(jnp.where(same_seq, earlier[None, :], -jnp.inf), axis=1)
            weight = jnp.exp(running - before)
            from_state = jnp.dot(readout_wide, state_in.T, precision=highest)
            projected = jnp.einsum("qn,rpn->rqp", readout_wide, head_init, precision=highest)
            from_init = jnp.sum(member_wide[:, :, None] * projected, axis=0)
            output = output + weight[:, None] * jnp.where(carried[:, None], from_state, from_init)
            last_weight = jnp.where(same_seq[-1], jnp.exp(running[-1] - running), 0.0)
            state_out = jnp.dot(
                (drive_block * last_weight[:, None]).T, basis_wide, precision=highest
            )
            init_last = jnp.einsum("r,rpn->pn", member_wide[:, -1], head_init, precision=highest)
            source = jnp.where(carried[-1], state_in, init_last)
            state_out = state_out + weight[-1] * source
            return (state_out, output)

        return jax.vmap(one_head)(states_in, drive_heads, decay_heads, init_heads)

    empty_state = jnp.zeros((local_heads, head_width, in_basis.shape[1]), jnp.float32)
    _, outputs = lax.scan(advance, empty_state, inputs)
    return outputs.transpose(0, 2, 1, 3).reshape(tokens_total, local_heads * head_width)


def local(
    resid_in,
    head_in,
    gate_in,
    in_basis,
    out_basis,
    step_size,
    decay_rate,
    init_state,
    lengths,
    norm_gain,
    out_proj,
    moe_gain,
    expert_ids,
    route_weight,
    placement,
    w_gate,
    w_up,
    w_down,
):
    tokens_total = head_in.shape[0]
    model_width = out_proj.shape[1]
    devices = lax.axis_size("mix")
    tok_rows = tokens_total // devices
    segment, first_of, member = request_layout(lengths, tokens_total)
    scan_out = scan_heads(
        head_in,
        step_size,
        decay_rate,
        in_basis,
        out_basis,
        init_state,
        segment,
        first_of,
        member,
        SPAN,
    )
    gated_out = scan_out * jax.nn.silu(gate_in.astype(jnp.float32))
    regrouped = lax.all_to_all(
        gated_out.astype(jnp.bfloat16), "mix", split_axis=0, concat_axis=1, tiled=True
    ).astype(gated_out.dtype)
    squares = jnp.sum(regrouped * regrouped, axis=1)
    mixed_in = (regrouped * norm_gain).astype(jnp.bfloat16)
    full_proj = lax.all_gather(out_proj, "mix", axis=0, tiled=True)
    group_terms = jnp.einsum(
        "tgc,gcd->tgd",
        mixed_in.reshape(tok_rows, devices, -1),
        full_proj.reshape(devices, -1, model_width),
        preferred_element_type=jnp.float32,
    ).astype(jnp.bfloat16)
    group_terms = lax.optimization_barrier(group_terms)
    mixer_sum = jnp.sum(group_terms.astype(jnp.float32), axis=1)
    mixer_out = mixer_sum * lax.rsqrt(squares / (HEADS * HEAD_DIM) + epsilon)[:, None]
    hidden = resid_in.astype(jnp.float32) + mixer_out
    normed = (
        hidden * lax.rsqrt(jnp.mean(hidden * hidden, axis=1, keepdims=True) + epsilon) * moe_gain
    ).astype(jnp.bfloat16)
    top_count = expert_ids.shape[1]
    flat_ids = expert_ids.reshape(-1)
    pair_count = flat_ids.shape[0]
    experts_total = placement.shape[0]
    cap_slots = 2 * pair_count // experts_total
    choose = (flat_ids[:, None] == jnp.arange(experts_total, dtype=jnp.int32)[None, :]).astype(
        jnp.int32
    )
    slot_of = jnp.sum(choose * placement[None, :], axis=1)
    slot_rank = jnp.sum(jnp.cumsum(choose, axis=0) * choose, axis=1) - 1
    buffer_index = slot_of * cap_slots + slot_rank
    owner_token = (
        jnp.full((experts_total * cap_slots,), -1, jnp.int32)
        .at[buffer_index]
        .set(jnp.arange(pair_count, dtype=jnp.int32) // top_count)
    )
    filled = owner_token >= 0
    send_rows = jnp.where(
        filled[:, None],
        jnp.take(normed, jnp.maximum(owner_token, 0), axis=0),
        jnp.zeros((), jnp.bfloat16),
    )
    send_rows = send_rows.reshape(devices, experts_total // devices, cap_slots, model_width)
    received = lax.all_to_all(send_rows, "mix", split_axis=0, concat_axis=0, tiled=True)
    gate_part = jnp.einsum("sekd,edf->sekf", received, w_gate, preferred_element_type=jnp.float32)
    up_part = jnp.einsum("sekd,edf->sekf", received, w_up, preferred_element_type=jnp.float32)
    inner_act = (jax.nn.silu(gate_part) * up_part).astype(jnp.bfloat16)
    result = jnp.einsum(
        "sekf,efd->sekd", inner_act, w_down, preferred_element_type=jnp.float32
    ).astype(jnp.bfloat16)
    returned_rows = lax.all_to_all(result, "mix", split_axis=0, concat_axis=0, tiled=True)
    back_flat = returned_rows.reshape(experts_total * cap_slots, model_width)
    picked = jnp.take(back_flat, buffer_index, axis=0).reshape(tok_rows, top_count, model_width)
    expert_sum = jnp.sum(route_weight[:, :, None] * picked.astype(jnp.float32), axis=1)
    return (hidden + expert_sum).astype(jnp.bfloat16)


def solution(mesh):
    return jax.shard_map(
        local,
        mesh=mesh,
        in_specs=(
            P(("groups", "mix"), None),
            P("groups", "mix"),
            P("groups", "mix"),
            P("groups", None),
            P("groups", None),
            P("mix", "groups"),
            P("mix"),
            P("groups", "mix", None, None),
            P("groups"),
            P(),
            P("mix", None),
            P(),
            P(("groups", "mix"), None),
            P(("groups", "mix"), None),
            P(),
            P("mix", None, None),
            P("mix", None, None),
            P("mix", None, None),
        ),
        out_specs=P(("groups", "mix"), None),
        check_vma=False,
    )
```

profile of v0, /device:TPU:15, one launch (start us, length us, event | category | flops | bytes accessed | tf_op | source)
XLA Modules:
  0.0 655.7 jit_solution(5398734231998708079)
XLA Ops:
  11.5 2.2 copy.110
  15.5 123.0 %while.13 = (s32[]{:T(128)}, f32[4,64,128]{2,1,0:T(8,128)S(1)}, f32[8,4,256,64]{2,3,1,0:T(8,128)}, f32[8,4,256,64]{2,0,3,1:T(8,128)}, s32[8,256]{1,0:T(8,128)S(1...) while((s32[]{:T(128)}, f32[4,64,128]{2,1,0:T(8,128)S(1)}, ...), condition=%wide.region_8.9_spmd.clone, body=%wide.region_3.8_spmd.clone.sunk | while | flops 1231164672 | bytes 6564249 | solution.py:110
  17.8 1.9 fusion.115
  23.2 1.8 constant_dynamic-slice_fusion.7
  25.0 2.2 fusion.116
  33.2 1.9 fusion.115
  38.6 1.8 constant_dynamic-slice_fusion.7
  40.4 2.1 fusion.116
  44.5 1.7 convolution_add_fusion.3
  48.6 1.9 fusion.115
  54.0 1.8 constant_dynamic-slice_fusion.7
  55.8 2.2 fusion.116
  64.0 1.9 fusion.115
  69.4 1.8 constant_dynamic-slice_fusion.7
  71.2 2.2 fusion.116
  75.3 1.7 convolution_add_fusion.3
  79.4 1.9 fusion.115
  84.8 1.8 constant_dynamic-slice_fusion.7
  86.6 2.2 fusion.116
  94.8 1.9 fusion.115
  100.1 1.8 constant_dynamic-slice_fusion.7
  101.9 2.1 fusion.116
  110.2 1.9 fusion.115
  115.5 1.8 constant_dynamic-slice_fusion.7
  117.3 2.1 fusion.116
  121.4 1.7 convolution_add_fusion.3
  125.5 1.9 fusion.115
  130.9 1.8 constant_dynamic-slice_fusion.7
  132.6 2.2 fusion.116
  138.5 2.9 copy.89
  143.8 1.9 fusion.62
  147.0 6.7 %all-to-all-start = ((bf16[16,128,256]{2,1,0:T(8,128)(2,1)}), bf16[16,128,256]{2,1,0:T(8,128)(2,1)S(1)}, u32[]{:S(2)}, u32[]{:S(2)}) async-start(bf16[16,128,256]{2,1,0:T(8,128)(2,1)} %bitcast.11), calls=%async_computation | async-start | bytes 2097152 | tf_op jit(solution)/shard_map/all_to_all | solution.py:152
  154.1 9.0 %reduce-window.26 = s32[32,8,128]{2,1,0:T(8,128)S(1)} reduce-window(s32[32,8,128]{2,1,0:T(8,128)S(1)} %fusion.68, s32[]{:T(128)} %constant.97.clone.1), window={size=1x1x128 pad=0_0x0_0x127_0}, to_apply=%region_12.13 | reduce-window | flops 4161536 | bytes 262148 | tf_op jit(solution)/shard_map/reduce-window.3
  163.7 4.3 scatter_custom_fusion
  168.2 10.4 %all-to-all-done = bf16[16,128,256]{2,1,0:T(8,128)(2,1)S(1)} async-done(((bf16[16,128,256]{2,1,0:T(8,128)(2,1)}), bf16[16,128,256]{2,1,0:T(8,128)(2,1)S(1)}, u32[]{:S(2)}, u32[]{:S(2)}) %all-to-all-start) | async-done | bytes 1048608 | tf_op jit(solution)/shard_map/all_to_all | solution.py:152
  178.9 11.4 %convert_bitcast_fusion.1 = bf16[128,16,2048]{2,0,1:T(8,128)(2,1)} fusion(bf16[16,256,2048]{2,1,0:T(8,128)(2,1)} %bitcast.224, bf16[16,128,256]{2,1,0:T(8,128)(2,1)S(1)} %all-to-all-done, f32[16,256]{1,0:T(8,128)S(1)} %mul.163), kind=kOutput, calls=%fused_computation.66 | convolution fusion | flops 2153250816 | bytes 26230784 | tf_op jit(solution)/shard_map/tgc,gcd->tgd/dot_general | solution.py:158
  190.3 5.3 convert_reduce_fusion
  196.3 11.0 %gather_fusion = bf16[2048,2048]{1,0:T(8,128)(2,1)} fusion(bf16[128,2048]{1,0:T(8,128)(2,1)S(1)} %multiply_convert_fusion, s32[2048]{0:T(1024)S(1)} %maximum_clamp_fusion), kind=kCustom, calls=%fused_computation | custom fusion | bytes 16785408 | tf_op jit(solution)/shard_map/jit(_take)/gather | solution.py:190
  207.3 4.6 select_select_fusion
  212.0 187.0 %all_to_all.23 = bf16[16,2,64,2048]{3,2,1,0:T(8,128)(2,1)S(1)} all-to-all(bf16[16,2,64,2048]{3,2,1,0:T(8,128)(2,1)S(1)} %select_select_fusion), channel_id=1, replica_groups=mesh['groups'=2,'mix'=16] {'mix'}, dimensions={0} | all-to-all | bytes 16777216 | tf_op jit(solution)/shard_map/all_to_all | solution.py:194
  398.9 10.6 %fusion.39 = f32[2,16,64,768]{3,2,1,0:T(8,128)} fusion(bf16[16,2,64,2048]{3,2,1,0:T(8,128)(2,1)S(1)} %all_to_all.23, bf16[2,2048,768]{2,1,0:T(8,128)(2,1)} %param.36), kind=kOutput, calls=%fused_computation.67 | convolution fusion | flops 6442450944 | bytes 20971520 | tf_op jit(solution)/shard_map/sekd,edf->sekf/dot_general | solution.py:196
  409.6 8.5 %fusion.41 = f32[2,16,64,768]{3,2,1,0:T(8,128)} fusion(bf16[16,2,64,2048]{3,2,1,0:T(8,128)(2,1)S(1)} %all_to_all.23, bf16[2,2048,768]{2,1,0:T(8,128)(2,1)S(1)} %bitcast.249), kind=kOutput, calls=%fused_computation.69 | convolution fusion | flops 6442450944 | bytes 20971520 | tf_op jit(solution)/shard_map/sekd,edf->sekf/dot_general | solution.py:195
  418.1 14.5 %convert_bitcast_fusion = bf16[16,2,64,2048]{3,2,0,1:T(8,128)(2,1)} fusion(bf16[2,768,2048]{2,1,0:T(8,128)(2,1)} %param.37, f32[2,16,64,768]{3,2,1,0:T(8,128)} %fusion.39, f32[2,16,64,768]{3,2,1,0:T(8,128)} %fusion.41), kind=kOutput, calls=%fused_computation.64 | convolution fusion | flops 6456082432 | bytes 27262976 | tf_op jit(solution)/shard_map/sekf,efd->sekd/dot_general | solution.py:198
  432.6 8.3 %copy.99 = bf16[16,2,64,2048]{3,2,1,0:T(8,128)(2,1)} copy(bf16[16,2,64,2048]{3,2,0,1:T(8,128)(2,1)} %convert_bitcast_fusion) | data formatting | bytes 16777216 | tf_op jit(solution)/shard_map/convert_element_type | solution.py:200
  440.8 5.7 all-to-all-start.2
  446.8 182.1 %all-to-all-done.2 = bf16[16,2,64,2048]{3,2,1,0:T(8,128)(2,1)} async-done(((bf16[16,2,64,2048]{3,2,1,0:T(8,128)(2,1)}), bf16[16,2,64,2048]{3,2,1,0:T(8,128)(2,1)}, u32[]{:S(2)}, u32[]{:S(2)}) %all-to-all-start.2) | async-done | bytes 8388640 | tf_op jit(solution)/shard_map/all_to_all | solution.py:201
  628.9 13.3 %gather_fusion.1 = bf16[1024,2048]{1,0:T(8,128)(2,1)} fusion(bf16[2048,2048]{1,0:T(8,128)(2,1)} %bitcast.29, s32[1024]{0:T(1024)S(1)} %broadcast_clamp_fusion), kind=kCustom, calls=%fused_computation.1 | custom fusion | bytes 8392704 | tf_op jit(solution)/shard_map/jit(_take)/gather | solution.py:203
  642.2 5.6 multiply_reduce_fusion
  (293 shorter events, 84.1 us)
Async XLA Ops:
  6.5 8.8 %copy-start.2 = (f32[4,2048]{1,0:T(4,128)S(1)}, f32[4,2048]{1,0:T(4,128)}, u32[]{:S(2)}) copy-start(f32[4,2048]{1,0:T(4,128)} %param.25) | copy-start | bytes 98308
  6.5 8.9 %copy-start.7 = (f32[4]{0:T(128)S(1)}, f32[4]{0:T(128)}, u32[]{:S(2)}) copy-start(f32[4]{0:T(128)} %param.26) | copy-start | bytes 52
  6.5 172.4 %all-gather.2.cloned.1.call-start = ((), (), s32[]{:S(2)}) async-start(), calls=%async_computation.3 | async-start | bytes 17825792 | tf_op jit(solution)/shard_map/all_gather | solution.py:157
  138.5 3.8 copy-start.1
  142.3 11.4 %copy-start.5 = (s32[128,8]{0,1:T(8,128)S(1)}, s32[128,8]{0,1:T(8,128)}, u32[]{:S(2)}) copy-start(s32[128,8]{0,1:T(8,128)} %param.32) | copy-start | bytes 12292
  142.3 11.7 %copy-start.3 = (f32[4096]{0:T(1024)S(1)}, f32[4096]{0:T(1024)}, u32[]{:S(2)}) copy-start(f32[4096]{0:T(1024)} %param.29) | copy-start | bytes 49156
  142.3 21.2 %copy-start.8 = (s32[32]{0:T(128)S(1)}, s32[32]{0:T(128)}, u32[]{:S(2)}) copy-start(s32[32]{0:T(128)} %param.34) | copy-start | bytes 388
  147.0 31.6 %all-to-all-start = ((bf16[16,128,256]{2,1,0:T(8,128)(2,1)}), bf16[16,128,256]{2,1,0:T(8,128)(2,1)S(1)}, u32[]{:S(2)}, u32[]{:S(2)}) async-start(bf16[16,128,256]{2,1,0:T(8,128)(2,1)} %bitcast.11), calls=%async_computation | async-start | bytes 2097152 | tf_op jit(solution)/shard_map/all_to_all | solution.py:152
  190.3 5.4 copy-start
  190.3 5.7 copy-start.4
  211.9 197.6 %slice-start = ((s8[6291456]{0:T(1024)(128)(4,1)}), s8[4194304]{0:T(1024)(128)(4,1)S(1)}, s32[]{:S(2)}) async-start(s8[6291456]{0:T(1024)(128)(4,1)} %bitcast.248), calls=%async_computation.4 | async-start | bytes 8388608
  398.9 10.6 %slice-start.1 = ((s8[6291456]{0:T(1024)(128)(4,1)}), s8[2097152]{0:T(1024)(128)(4,1)S(1)}, s32[]{:S(2)}) async-start(s8[6291456]{0:T(1024)(128)(4,1)} %bitcast.248), calls=%async_computation.5 | async-start | bytes 4194304
  440.8 5.8 copy-start.6
  440.8 188.1 %all-to-all-start.2 = ((bf16[16,2,64,2048]{3,2,1,0:T(8,128)(2,1)}), bf16[16,2,64,2048]{3,2,1,0:T(8,128)(2,1)}, u32[]{:S(2)}, u32[]{:S(2)}) async-start(bf16[16,2,64,2048]{3,2,1,0:T(8,128)(2,1)} %copy.99), calls=%async_computation.2 | async-start | bytes 16777216 | tf_op jit(solution)/shard_map/all_to_all | solution.py:201
Sparse Core Ops, SparseCore 0:
  9.5 125.3 all-gather.1
where the time goes:
time: 658 us; the launch traced here: 656 us
  waiting for transfers between devices  193 us (29%)
  blocking collectives  187 us (28%)
  matrix products  118 us (18%)
  local copies, waits for them, and re-layouts  79.6 us (12%)
  other arithmetic  51.1 us (8%)
  between operations  13.8 us (2%)
  starting transfers between devices  12.5 us (2%)
    all_to_all x1, blocking collectives, local(): lax.all_to_all(send_rows, 'mix', split_axis=0, concat_axis=0, tiled=True)  187 us
    all_to_all x1, waiting for transfers between devices, local(): lax.all_to_all(result, 'mix', split_axis=0, concat_axis=0, tiled=True)  182 us
    another operation x20, other arithmetic  20.1 us
    dynamic_slice x32, local copies, waits for them, and re-layouts, scan_heads(): _, outputs = lax.scan(advance, empty_state, inputs)  19.4 us
    dot_general x8, matrix products, one_head(): output = jnp.dot(kernel * scores, drive_block, precision=highest)  17.2 us
    dot_general x8, matrix products, one_head(): jnp.einsum('qn,rpn->rqp', readout_wide, head_init, precision=highest)  14.9 us
    dot_general x1, matrix products, local(): jnp.einsum('sekf,efd->sekd', inner_act, w_down, preferred_element_type=jn...  14.5 us
    dot_general x8, matrix products, one_head(): jnp.dot((drive_block * last_weight[:, None]).T, basis_wide, precision=hig...  13.8 us
  transfers between devices with their start and end apart: 3, of which 2 were waited for; matrix products, arithmetic and copies ran while one was open for 23% of the time, Pallas kernels for 0%

commit v1 on v0

--- a/solution.py
+++ b/solution.py
@@ -198,7 +198,20 @@
     result = jnp.einsum(
         "sekf,efd->sekd", inner_act, w_down, preferred_element_type=jnp.float32
     ).astype(jnp.bfloat16)
-    returned_rows = lax.all_to_all(result, "mix", split_axis=0, concat_axis=0, tiled=True)
+    moved, answer = (lax.axis_size("mix"), lax.axis_index("mix"))
+    tmp = list(result.shape)
+    z_new = result.shape[0] // moved
+    tmp[0] = z_new
+    now = tmp[0]
+    tmp[0] = now * moved
+    returned_rows = jnp.zeros(tmp, result.dtype)
+    for h in range(moved):
+        a_next = lax.dynamic_slice_in_dim(result, (answer ^ h) * z_new, z_new, axis=0)
+        if h:
+            a_next = lax.ppermute(a_next, "mix", tuple(((i, i ^ h) for i in range(moved))))
+        returned_rows = lax.dynamic_update_slice_in_dim(
+            returned_rows, a_next, (answer ^ h) * now, axis=0
+        )
     back_flat = returned_rows.reshape(experts_total * cap_slots, model_width)
     picked = jnp.take(back_flat, buffer_index, axis=0).reshape(tok_rows, top_count, model_width)
     expert_sum = jnp.sum(route_weight[:, :, None] * picked.astype(jnp.float32), axis=1)

time: 658 us -> 687 us (1.044)
  blocking collectives: 187 us -> 0 us
  waiting for transfers between devices: 193 us -> 365 us
  local copies, waits for them, and re-layouts: 79.6 us -> 98.4 us
  starting transfers between devices: 12.5 us -> 27.5 us
    all_to_all x1 -> x0, blocking collectives: 187 us -> none  [local(): lax.all_to_all(send_rows, 'mix', split_axis=0, concat_axis=0, tiled=True)]
    ppermute x0 -> x15, waiting for transfers between devices: none -> 172 us  [local(): lax.ppermute(a_next, 'mix', tuple(((i, i ^ h) for i in range(moved))))]
    dynamic_update_slice x0 -> x16, local copies, waits for them, and re-layouts: none -> 16.7 us  [local(): lax.dynamic_update_slice_in_dim(returned_rows, a_next, (answer ^ h) * now...]
    ppermute x0 -> x15, starting transfers between devices: none -> 15.9 us  [local(): lax.ppermute(a_next, 'mix', tuple(((i, i ^ h) for i in range(moved))))]
    convert_element_type x1 -> x0, local copies, waits for them, and re-layouts: 8.25 us -> none  [local(): result = jnp.einsum('sekf,efd->sekd', inner_act, w_down, preferred_elemen...]
  transfers between devices with their start and end apart: 3 -> 18, of which waited for: 2 -> 12; matrix products, arithmetic and copies ran while one was open for 23% -> 25% of each run, Pallas kernels for 0% -> 0%
where the time goes in v1:
time: 687 us; the launch traced here: 684 us
  waiting for transfers between devices  365 us (53%)
  matrix products  124 us (18%)
  local copies, waits for them, and re-layouts  98.4 us (14%)
  other arithmetic  53.9 us (8%)
  starting transfers between devices  27.5 us (4%)
  between operations  14 us (2%)
    all_to_all x1, waiting for transfers between devices, local(): lax.all_to_all(send_rows, 'mix', split_axis=0, concat_axis=0, tiled=True)  182 us
    ppermute x15, waiting for transfers between devices, local(): lax.ppermute(a_next, 'mix', tuple(((i, i ^ h) for i in range(moved))))  172 us
    another operation x20, other arithmetic  20.1 us
    dynamic_slice x32, local copies, waits for them, and re-layouts, scan_heads(): _, outputs = lax.scan(advance, empty_state, inputs)  19.4 us
    dot_general x8, matrix products, one_head(): output = jnp.dot(kernel * scores, drive_block, precision=highest)  17.2 us
    dynamic_update_slice x16, local copies, waits for them, and re-layouts, local(): lax.dynamic_update_slice_in_dim(returned_rows, a_next, (answer ^ h) * now...  16.7 us
    ppermute x15, starting transfers between devices, local(): lax.ppermute(a_next, 'mix', tuple(((i, i ^ h) for i in range(moved))))  15.9 us
    dot_general x8, matrix products, one_head(): jnp.einsum('qn,rpn->rqp', readout_wide, head_init, precision=highest)  14.9 us
  transfers between devices with their start and end apart: 18, of which 12 were waited for; matrix products, arithmetic and copies ran while one was open for 25% of the time, Pallas kernels for 0%

profile of v1, /device:TPU:15, one launch (start us, length us, event | category | flops | bytes accessed | tf_op | source)
XLA Modules:
  0.0 683.6 jit_solution(5360304544563115784)
XLA Ops:
  11.5 2.2 copy.107
  15.5 123.0 %while.13 = (s32[]{:T(128)}, f32[4,64,128]{2,1,0:T(8,128)S(1)}, f32[8,4,256,64]{2,3,1,0:T(8,128)}, f32[8,4,256,64]{2,0,3,1:T(8,128)}, s32[8,256]{1,0:T(8,128)S(1...) while((s32[]{:T(128)}, f32[4,64,128]{2,1,0:T(8,128)S(1)}, ...), condition=%wide.region_8.9_spmd.clone, body=%wide.region_3.8_spmd.clone.sunk | while | flops 1231164672 | bytes 6564249 | solution.py:110
  17.8 1.9 fusion.116
  25.0 2.2 fusion.117
  40.4 2.1 fusion.117
  48.6 1.9 fusion.116
  55.8 2.2 fusion.117
  64.0 1.9 fusion.116
  71.2 2.2 fusion.117
  79.4 1.9 fusion.116
  86.6 2.2 fusion.117
  94.8 1.9 fusion.116
  101.9 2.1 fusion.117
  117.3 2.1 fusion.117
  125.5 1.9 fusion.116
  132.6 2.2 fusion.117
  138.5 2.9 copy.87
  147.0 6.7 all-to-all-start
  154.1 9.0 %reduce-window.26 = s32[32,8,128]{2,1,0:T(8,128)S(1)} reduce-window(s32[32,8,128]{2,1,0:T(8,128)S(1)} %fusion.69, s32[]{:T(128)} %constant.66.clone.1), window={size=1x1x128 pad=0_0x0_0x127_0}, to_apply=%region_12.13 | reduce-window | flops 4161536 | bytes 262148 | tf_op jit(solution)/shard_map/reduce-window.3
  163.7 4.3 scatter_custom_fusion
  168.2 10.4 %all-to-all-done = bf16[16,128,256]{2,1,0:T(8,128)(2,1)S(1)} async-done(((bf16[16,128,256]{2,1,0:T(8,128)(2,1)}), bf16[16,128,256]{2,1,0:T(8,128)(2,1)S(1)}, u32[]{:S(2)}, u32[]{:S(2)}) %all-to-all-start) | async-done | bytes 1048608 | tf_op jit(solution)/shard_map/all_to_all | solution.py:152
  178.9 11.4 %convert_bitcast_fusion = bf16[128,16,2048]{2,0,1:T(8,128)(2,1)} fusion(bf16[16,256,2048]{2,1,0:T(8,128)(2,1)} %bitcast.254, bf16[16,128,256]{2,1,0:T(8,128)(2,1)S(1)} %all-to-all-done, f32[16,256]{1,0:T(8,128)S(1)} %mul.163), kind=kOutput, calls=%fused_computation.65 | convolution fusion | flops 2153250816 | bytes 26230784 | tf_op jit(solution)/shard_map/tgc,gcd->tgd/dot_general | solution.py:158
  190.3 5.3 convert_reduce_fusion
  196.3 11.0 %gather_fusion = bf16[2048,2048]{1,0:T(8,128)(2,1)} fusion(bf16[128,2048]{1,0:T(8,128)(2,1)S(1)} %multiply_convert_fusion, s32[2048]{0:T(1024)S(1)} %maximum_clamp_fusion), kind=kCustom, calls=%fused_computation | custom fusion | bytes 16785408 | tf_op jit(solution)/shard_map/jit(_take)/gather | solution.py:190
  207.3 7.4 %select_select_fusion = bf16[16,2,64,2048]{3,2,1,0:T(8,128)(2,1)} fusion(bf16[16,2,64,2048]{3,2,1,0:T(8,128)(2,1)} %bitcast.255, pred[16,2,64]{2,1,0:T(4,128)(4,1)S(1)} %broadcast_in_dim.139, pred[16,2,64]{2,1,0:T(4,128)(4,1)S(1)} %broadcast_in_dim.137), kind=kLoop, calls=%fused_computation.64 | loop fusion | flops 8388608 | bytes 16781312 | tf_op jit(solution)/shard_map/jit(_where)/select_n | solution.py:188
  214.7 4.9 all-to-all-start.1
  219.8 182.1 %all-to-all-done.1 = bf16[16,2,64,2048]{3,2,1,0:T(8,128)(2,1)} async-done(((bf16[16,2,64,2048]{3,2,1,0:T(8,128)(2,1)}), bf16[16,2,64,2048]{3,2,1,0:T(8,128)(2,1)}, u32[]{:S(2)}, u32[]{:S(2)}) %all-to-all-start.1) | async-done | bytes 8388640 | tf_op jit(solution)/shard_map/all_to_all | solution.py:194
  401.9 12.7 %fusion.39 = f32[2,16,64,768]{3,2,1,0:T(8,128)} fusion(bf16[16,2,64,2048]{3,2,1,0:T(8,128)(2,1)} %all-to-all-done.1, bf16[2,2048,768]{2,1,0:T(8,128)(2,1)} %param.36), kind=kOutput, calls=%fused_computation.66 | convolution fusion | flops 6442450944 | bytes 20971520 | tf_op jit(solution)/shard_map/sekd,edf->sekf/dot_general | solution.py:196
  414.6 12.6 %fusion.41 = f32[2,16,64,768]{3,2,1,0:T(8,128)} fusion(bf16[16,2,64,2048]{3,2,1,0:T(8,128)(2,1)} %all-to-all-done.1, bf16[2,2048,768]{2,1,0:T(8,128)(2,1)} %param.35), kind=kOutput, calls=%fused_computation.68 | convolution fusion | flops 6442450944 | bytes 20971520 | tf_op jit(solution)/shard_map/sekd,edf->sekf/dot_general | solution.py:195
  427.1 14.5 %fusion.51 = bf16[2,16,64,2048]{3,2,1,0:T(8,128)(2,1)} fusion(bf16[2,768,2048]{2,1,0:T(8,128)(2,1)} %param.37, f32[2,16,64,768]{3,2,1,0:T(8,128)} %fusion.39, f32[2,16,64,768]{3,2,1,0:T(8,128)} %fusion.41), kind=kOutput, calls=%fused_computation.81 | convolution fusion | flops 6456082432 | bytes 27262976 | tf_op jit(solution)/shard_map/sekf,efd->sekd/dot_general | solution.py:198
  441.7 6.1 dynamic-slice_bitcast_fusion.1
  448.1 2.1 collective-permute-start.2
  451.7 4.3 broadcast_in_dim.135
  455.9 1.9 bitcast_dynamic-update-slice_fusion
  457.9 1.9 constant_dynamic-update-slice_fusion.13
  462.7 1.9 constant_dynamic-update-slice_fusion.12
  464.6 8.7 %collective-permute-done.2 = bf16[1,2,64,2048]{3,2,1,0:T(8,128)(2,1)S(1)} collective-permute-done((bf16[1,2,64,2048]{3,2,1,0:T(8,128)(2,1)}, bf16[1,2,64,2048]{3,2,1,0:T(8,128)(2,1)S(1)}, u32[]{:S(2)}, u32[]{:S(2)}) %collective-permute-start.2) | collective-permute-done | bytes 524320 | tf_op jit(solution)/shard_map/ppermute | solution.py:211
  479.1 28.3 %collective-permute-done.5 = bf16[1,2,64,2048]{3,2,1,0:T(8,128)(2,1)S(1)} collective-permute-done((bf16[1,2,64,2048]{3,2,1,0:T(8,128)(2,1)S(1)}, bf16[1,2,64,2048]{3,2,1,0:T(8,128)(2,1)S(1)}, u32[]{:S(2)}, u32[]{:S(2)}) %collective-permute-start.5) | collective-permute-done | bytes 524320 | tf_op jit(solution)/shard_map/ppermute | solution.py:211
  507.4 4.2 collective-permute-start.10
  512.5 6.1 collective-permute-done.6
  523.6 63.7 %collective-permute-done.9 = bf16[1,2,64,2048]{3,2,1,0:T(8,128)(2,1)S(1)} collective-permute-done((bf16[1,2,64,2048]{3,2,1,0:T(8,128)(2,1)S(1)}, bf16[1,2,64,2048]{3,2,1,0:T(8,128)(2,1)S(1)}, u32[]{:S(2)}, u32[]{:S(2)}) %collective-permute-start.9) | collective-permute-done | bytes 524320 | tf_op jit(solution)/shard_map/ppermute | solution.py:211
  589.1 20.7 %collective-permute-done.10 = bf16[1,2,64,2048]{3,2,1,0:T(8,128)(2,1)S(1)} collective-permute-done((bf16[1,2,64,2048]{3,2,1,0:T(8,128)(2,1)S(1)}, bf16[1,2,64,2048]{3,2,1,0:T(8,128)(2,1)S(1)}, u32[]{:S(2)}, u32[]{:S(2)}) %collective-permute-start.10) | collective-permute-done | bytes 524320 | tf_op jit(solution)/shard_map/ppermute | solution.py:211
  610.7 10.4 %collective-permute-done.11 = bf16[1,2,64,2048]{3,2,1,0:T(8,128)(2,1)S(1)} collective-permute-done((bf16[1,2,64,2048]{3,2,1,0:T(8,128)(2,1)S(1)}, bf16[1,2,64,2048]{3,2,1,0:T(8,128)(2,1)S(1)}, u32[]{:S(2)}, u32[]{:S(2)}) %collective-permute-start.11) | collective-permute-done | bytes 524320 | tf_op jit(solution)/shard_map/ppermute | solution.py:211
  621.9 10.6 %collective-permute-done.12 = bf16[1,2,64,2048]{3,2,1,0:T(8,128)(2,1)S(1)} collective-permute-done((bf16[1,2,64,2048]{3,2,1,0:T(8,128)(2,1)S(1)}, bf16[1,2,64,2048]{3,2,1,0:T(8,128)(2,1)S(1)}, u32[]{:S(2)}, u32[]{:S(2)}) %collective-permute-start.12) | collective-permute-done | bytes 524320 | tf_op jit(solution)/shard_map/ppermute | solution.py:211
  633.3 11.4 %collective-permute-done.13 = bf16[1,2,64,2048]{3,2,1,0:T(8,128)(2,1)S(1)} collective-permute-done((bf16[1,2,64,2048]{3,2,1,0:T(8,128)(2,1)S(1)}, bf16[1,2,64,2048]{3,2,1,0:T(8,128)(2,1)S(1)}, u32[]{:S(2)}, u32[]{:S(2)}) %collective-permute-start.13) | collective-permute-done | bytes 524320 | tf_op jit(solution)/shard_map/ppermute | solution.py:211
  645.6 10.4 %collective-permute-done.14 = bf16[1,2,64,2048]{3,2,1,0:T(8,128)(2,1)S(1)} collective-permute-done((bf16[1,2,64,2048]{3,2,1,0:T(8,128)(2,1)S(1)}, bf16[1,2,64,2048]{3,2,1,0:T(8,128)(2,1)S(1)}, u32[]{:S(2)}, u32[]{:S(2)}) %collective-permute-start.14) | collective-permute-done | bytes 524320 | tf_op jit(solution)/shard_map/ppermute | solution.py:211
  656.8 13.3 %gather_fusion.1 = bf16[1024,2048]{1,0:T(8,128)(2,1)} fusion(bf16[2048,2048]{1,0:T(8,128)(2,1)} %bitcast.44, s32[1024]{0:T(1024)S(1)} %broadcast_clamp_fusion), kind=kCustom, calls=%fused_computation.1 | custom fusion | bytes 8392704 | tf_op jit(solution)/shard_map/jit(_take)/gather | solution.py:216
  670.1 5.6 multiply_reduce_fusion
  (348 shorter events, 131.4 us)
Async XLA Ops:
  6.5 8.8 %copy-start.9 = (f32[4,2048]{1,0:T(4,128)S(1)}, f32[4,2048]{1,0:T(4,128)}, u32[]{:S(2)}) copy-start(f32[4,2048]{1,0:T(4,128)} %param.25) | copy-start | bytes 98308
  6.5 8.9 %copy-start.14 = (f32[4]{0:T(128)S(1)}, f32[4]{0:T(128)}, u32[]{:S(2)}) copy-start(f32[4]{0:T(128)} %param.26) | copy-start | bytes 52
  6.5 172.4 %all-gather.2.cloned.1.call-start = ((), (), s32[]{:S(2)}) async-start(), calls=%async_computation.2 | async-start | bytes 17825792 | tf_op jit(solution)/shard_map/all_gather | solution.py:157
  138.5 3.8 copy-start.1
  141.4 12.3 %copy-start.12 = (s32[128,8]{0,1:T(8,128)S(1)}, s32[128,8]{0,1:T(8,128)}, u32[]{:S(2)}) copy-start(s32[128,8]{0,1:T(8,128)} %param.32) | copy-start | bytes 12292
  141.4 12.6 %copy-start.10 = (f32[4096]{0:T(1024)S(1)}, f32[4096]{0:T(1024)}, u32[]{:S(2)}) copy-start(f32[4096]{0:T(1024)} %param.29) | copy-start | bytes 49156
  141.4 22.1 %copy-start.15 = (s32[32]{0:T(128)S(1)}, s32[32]{0:T(128)}, u32[]{:S(2)}) copy-start(s32[32]{0:T(128)} %param.34) | copy-start | bytes 388
  147.0 31.6 %all-to-all-start = ((bf16[16,128,256]{2,1,0:T(8,128)(2,1)}), bf16[16,128,256]{2,1,0:T(8,128)(2,1)S(1)}, u32[]{:S(2)}, u32[]{:S(2)}) async-start(bf16[16,128,256]{2,1,0:T(8,128)(2,1)} %bitcast.11), calls=%async_computation | async-start | bytes 2097152 | tf_op jit(solution)/shard_map/all_to_all | solution.py:152
  190.3 5.4 copy-start
  190.3 5.7 copy-start.11
  214.7 187.2 %all-to-all-start.1 = ((bf16[16,2,64,2048]{3,2,1,0:T(8,128)(2,1)}), bf16[16,2,64,2048]{3,2,1,0:T(8,128)(2,1)}, u32[]{:S(2)}, u32[]{:S(2)}) async-start(bf16[16,2,64,2048]{3,2,1,0:T(8,128)(2,1)} %select_select_fusion), calls=%async_computation.1 | async-start | bytes 16777216 | tf_op jit(solution)/shard_map/all_to_all | solution.py:194
  441.7 6.3 copy-start.13
  447.7 10.1 %collective-permute-start = (bf16[1,2,64,2048]{3,2,1,0:T(8,128)(2,1)}, bf16[1,2,64,2048]{3,2,1,0:T(8,128)(2,1)}, u32[]{:S(2)}, u32[]{:S(2)}) collective-permute-start(bf16[1,2,64,2048]{3,2,1,0:T(8,128)(2,1)} %get-tuple-element.208), channel_id=1, source_target_pairs={{0,1},{1,0},{2,3},{3,2},{4,5},{5,4},{6,7},{7,6},{8,9},{9,8},{10,11... | collective-permute-start | bytes 1572872 | tf_op jit(solution)/shard_map/ppermute | solution.py:211
  447.9 13.5 %collective-permute-start.1 = (bf16[1,2,64,2048]{3,2,1,0:T(8,128)(2,1)}, bf16[1,2,64,2048]{3,2,1,0:T(8,128)(2,1)}, u32[]{:S(2)}, u32[]{:S(2)}) collective-permute-start(bf16[1,2,64,2048]{3,2,1,0:T(8,128)(2,1)} %get-tuple-element.207), channel_id=1, source_target_pairs={{0,2},{1,3},{2,0},{3,1},{4,6},{5,7},{6,4},{7,5},{8,10},{9,11},{10,... | collective-permute-start | bytes 1572872 | tf_op jit(solution)/shard_map/ppermute | solution.py:211
  448.1 9.8 %copy-start.8 = (bf16[1,2,64,2048]{3,2,1,0:T(8,128)(2,1)S(1)}, bf16[1,2,64,2048]{3,2,1,0:T(8,128)(2,1)}, u32[]{:S(2)}) copy-start(bf16[1,2,64,2048]{3,2,1,0:T(8,128)(2,1)} %get-tuple-element.203) | copy-start | bytes 1572868
  448.1 13.3 %copy-start.7 = (bf16[1,2,64,2048]{3,2,1,0:T(8,128)(2,1)S(1)}, bf16[1,2,64,2048]{3,2,1,0:T(8,128)(2,1)}, u32[]{:S(2)}) copy-start(bf16[1,2,64,2048]{3,2,1,0:T(8,128)(2,1)} %get-tuple-element.202) | copy-start | bytes 1572868
  448.1 25.2 %copy-start.6 = (bf16[1,2,64,2048]{3,2,1,0:T(8,128)(2,1)S(1)}, bf16[1,2,64,2048]{3,2,1,0:T(8,128)(2,1)}, u32[]{:S(2)}) copy-start(bf16[1,2,64,2048]{3,2,1,0:T(8,128)(2,1)} %get-tuple-element.201) | copy-start | bytes 1572868
  448.1 27.2 %copy-start.5 = (bf16[1,2,64,2048]{3,2,1,0:T(8,128)(2,1)S(1)}, bf16[1,2,64,2048]{3,2,1,0:T(8,128)(2,1)}, u32[]{:S(2)}) copy-start(bf16[1,2,64,2048]{3,2,1,0:T(8,128)(2,1)} %get-tuple-element.200) | copy-start | bytes 1572868
  448.1 29.0 %copy-start.4 = (bf16[1,2,64,2048]{3,2,1,0:T(8,128)(2,1)S(1)}, bf16[1,2,64,2048]{3,2,1,0:T(8,128)(2,1)}, u32[]{:S(2)}) copy-start(bf16[1,2,64,2048]{3,2,1,0:T(8,128)(2,1)} %get-tuple-element.199) | copy-start | bytes 1572868
  448.1 59.3 %copy-start.3 = (bf16[1,2,64,2048]{3,2,1,0:T(8,128)(2,1)S(1)}, bf16[1,2,64,2048]{3,2,1,0:T(8,128)(2,1)}, u32[]{:S(2)}) copy-start(bf16[1,2,64,2048]{3,2,1,0:T(8,128)(2,1)} %get-tuple-element.198) | copy-start | bytes 1572868
  448.1 70.5 %copy-start.2 = (bf16[1,2,64,2048]{3,2,1,0:T(8,128)(2,1)S(1)}, bf16[1,2,64,2048]{3,2,1,0:T(8,128)(2,1)}, u32[]{:S(2)}) copy-start(bf16[1,2,64,2048]{3,2,1,0:T(8,128)(2,1)} %get-tuple-element.197) | copy-start | bytes 1572868
  448.1 25.2 %collective-permute-start.2 = (bf16[1,2,64,2048]{3,2,1,0:T(8,128)(2,1)}, bf16[1,2,64,2048]{3,2,1,0:T(8,128)(2,1)S(1)}, u32[]{:S(2)}, u32[]{:S(2)}) collective-permute-start(bf16[1,2,64,2048]{3,2,1,0:T(8,128)(2,1)} %get-tuple-element.206), channel_id=1, source_target_pairs={{0,3},{1,2},{2,1},{3,0},{4,7},{5,6},{6,5},{7,4},{8,11},{9,10},{10,... | collective-permute-start | bytes 1572872 | tf_op jit(solution)/shard_map/ppermute | solution.py:211
  450.2 25.1 %collective-permute-start.3 = (bf16[1,2,64,2048]{3,2,1,0:T(8,128)(2,1)}, bf16[1,2,64,2048]{3,2,1,0:T(8,128)(2,1)S(1)}, u32[]{:S(2)}, u32[]{:S(2)}) collective-permute-start(bf16[1,2,64,2048]{3,2,1,0:T(8,128)(2,1)} %get-tuple-element.205), channel_id=1, source_target_pairs={{0,4},{1,5},{2,6},{3,7},{4,0},{5,1},{6,2},{7,3},{8,12},{9,13},{10,... | collective-permute-start | bytes 1572872 | tf_op jit(solution)/shard_map/ppermute | solution.py:211
  450.2 26.9 %collective-permute-start.4 = (bf16[1,2,64,2048]{3,2,1,0:T(8,128)(2,1)}, bf16[1,2,64,2048]{3,2,1,0:T(8,128)(2,1)S(1)}, u32[]{:S(2)}, u32[]{:S(2)}) collective-permute-start(bf16[1,2,64,2048]{3,2,1,0:T(8,128)(2,1)} %get-tuple-element.204), channel_id=1, source_target_pairs={{0,5},{1,4},{2,7},{3,6},{4,1},{5,0},{6,3},{7,2},{8,13},{9,12},{10,... | collective-permute-start | bytes 1572872 | tf_op jit(solution)/shard_map/ppermute | solution.py:211
  457.8 49.5 %collective-permute-start.5 = (bf16[1,2,64,2048]{3,2,1,0:T(8,128)(2,1)S(1)}, bf16[1,2,64,2048]{3,2,1,0:T(8,128)(2,1)S(1)}, u32[]{:S(2)}, u32[]{:S(2)}) collective-permute-start(bf16[1,2,64,2048]{3,2,1,0:T(8,128)(2,1)S(1)} %copy-done.8), channel_id=1, source_target_pairs={{0,6},{1,7},{2,4},{3,5},{4,2},{5,3},{6,0},{7,1},{8,14},{9,15},{10,... | collective-permute-start | bytes 1572872 | tf_op jit(solution)/shard_map/ppermute | solution.py:211
  461.3 57.3 %collective-permute-start.6 = (bf16[1,2,64,2048]{3,2,1,0:T(8,128)(2,1)S(1)}, bf16[1,2,64,2048]{3,2,1,0:T(8,128)(2,1)S(1)}, u32[]{:S(2)}, u32[]{:S(2)}) collective-permute-start(bf16[1,2,64,2048]{3,2,1,0:T(8,128)(2,1)S(1)} %copy-done.7), channel_id=1, source_target_pairs={{0,7},{1,6},{2,5},{3,4},{4,3},{5,2},{6,1},{7,0},{8,15},{9,14},{10,... | collective-permute-start | bytes 1572872 | tf_op jit(solution)/shard_map/ppermute | solution.py:211
  473.3 46.7 %collective-permute-start.7 = (bf16[1,2,64,2048]{3,2,1,0:T(8,128)(2,1)S(1)}, bf16[1,2,64,2048]{3,2,1,0:T(8,128)(2,1)S(1)}, u32[]{:S(2)}, u32[]{:S(2)}) collective-permute-start(bf16[1,2,64,2048]{3,2,1,0:T(8,128)(2,1)S(1)} %copy-done.6), channel_id=1, source_target_pairs={{0,8},{1,9},{2,10},{3,11},{4,12},{5,13},{6,14},{7,15},{8,0},{9,1},... | collective-permute-start | bytes 1572872 | tf_op jit(solution)/shard_map/ppermute | solution.py:211
  475.3 47.0 %collective-permute-start.8 = (bf16[1,2,64,2048]{3,2,1,0:T(8,128)(2,1)S(1)}, bf16[1,2,64,2048]{3,2,1,0:T(8,128)(2,1)S(1)}, u32[]{:S(2)}, u32[]{:S(2)}) collective-permute-start(bf16[1,2,64,2048]{3,2,1,0:T(8,128)(2,1)S(1)} %copy-done.5), channel_id=1, source_target_pairs={{0,9},{1,8},{2,11},{3,10},{4,13},{5,12},{6,15},{7,14},{8,1},{9,0},... | collective-permute-start | bytes 1572872 | tf_op jit(solution)/shard_map/ppermute | solution.py:211
  477.1 110.3 %collective-permute-start.9 = (bf16[1,2,64,2048]{3,2,1,0:T(8,128)(2,1)S(1)}, bf16[1,2,64,2048]{3,2,1,0:T(8,128)(2,1)S(1)}, u32[]{:S(2)}, u32[]{:S(2)}) collective-permute-start(bf16[1,2,64,2048]{3,2,1,0:T(8,128)(2,1)S(1)} %copy-done.4), channel_id=1, source_target_pairs={{0,10},{1,11},{2,8},{3,9},{4,14},{5,15},{6,12},{7,13},{8,2},{9,3},... | collective-permute-start | bytes 1572872 | tf_op jit(solution)/shard_map/ppermute | solution.py:211
  507.4 102.5 %collective-permute-start.10 = (bf16[1,2,64,2048]{3,2,1,0:T(8,128)(2,1)S(1)}, bf16[1,2,64,2048]{3,2,1,0:T(8,128)(2,1)S(1)}, u32[]{:S(2)}, u32[]{:S(2)}) collective-permute-start(bf16[1,2,64,2048]{3,2,1,0:T(8,128)(2,1)S(1)} %copy-done.3), channel_id=1, source_target_pairs={{0,11},{1,10},{2,9},{3,8},{4,15},{5,14},{6,13},{7,12},{8,3},{9,2},... | collective-permute-start | bytes 1572872 | tf_op jit(solution)/shard_map/ppermute | solution.py:211
  518.6 102.5 %collective-permute-start.11 = (bf16[1,2,64,2048]{3,2,1,0:T(8,128)(2,1)S(1)}, bf16[1,2,64,2048]{3,2,1,0:T(8,128)(2,1)S(1)}, u32[]{:S(2)}, u32[]{:S(2)}) collective-permute-start(bf16[1,2,64,2048]{3,2,1,0:T(8,128)(2,1)S(1)} %copy-done.2), channel_id=1, source_target_pairs={{0,12},{1,13},{2,14},{3,15},{4,8},{5,9},{6,10},{7,11},{8,4},{9,5},... | collective-permute-start | bytes 1572872 | tf_op jit(solution)/shard_map/ppermute | solution.py:211
  520.0 112.5 %collective-permute-start.12 = (bf16[1,2,64,2048]{3,2,1,0:T(8,128)(2,1)S(1)}, bf16[1,2,64,2048]{3,2,1,0:T(8,128)(2,1)S(1)}, u32[]{:S(2)}, u32[]{:S(2)}) collective-permute-start(bf16[1,2,64,2048]{3,2,1,0:T(8,128)(2,1)S(1)} %get-tuple-element.196), channel_id=1, source_target_pairs={{0,13},{1,12},{2,15},{3,14},{4,9},{5,8},{6,11},{7,10},{8,5},{9,4},... | collective-permute-start | bytes 1572872 | tf_op jit(solution)/shard_map/ppermute | solution.py:211
  522.4 122.4 %collective-permute-start.13 = (bf16[1,2,64,2048]{3,2,1,0:T(8,128)(2,1)S(1)}, bf16[1,2,64,2048]{3,2,1,0:T(8,128)(2,1)S(1)}, u32[]{:S(2)}, u32[]{:S(2)}) collective-permute-start(bf16[1,2,64,2048]{3,2,1,0:T(8,128)(2,1)S(1)} %get-tuple-element.195), channel_id=1, source_target_pairs={{0,14},{1,15},{2,12},{3,13},{4,10},{5,11},{6,8},{7,9},{8,6},{9,7},... | collective-permute-start | bytes 1572872 | tf_op jit(solution)/shard_map/ppermute | solution.py:211
  587.4 68.6 %collective-permute-start.14 = (bf16[1,2,64,2048]{3,2,1,0:T(8,128)(2,1)S(1)}, bf16[1,2,64,2048]{3,2,1,0:T(8,128)(2,1)S(1)}, u32[]{:S(2)}, u32[]{:S(2)}) collective-permute-start(bf16[1,2,64,2048]{3,2,1,0:T(8,128)(2,1)S(1)} %get-tuple-element.194), channel_id=1, source_target_pairs={{0,15},{1,14},{2,13},{3,12},{4,11},{5,10},{6,9},{7,8},{8,7},{9,6},... | collective-permute-start | bytes 1572872 | tf_op jit(solution)/shard_map/ppermute | solution.py:211
Sparse Core Ops, SparseCore 0:
  9.5 125.3 all-gather.1
